TPU v7x, 32 devices: a whole 2x2x4 slice. The times are simulated.
32 devices in a mesh: dp: 8 (over y, x, core), tensor: 4 (over z).
Axes of the slice: x: 2, y: 2, z: 4, core: 2. Of those that a mesh axis runs over, the one named last changes fastest.
Arguments:
- tokens: bfloat16 [8192, 2048], P(('dp', 'tensor')), may hold values from -6 to 6
- lengths: int32 [8], P('dp'), may hold values from 256 to 1024, as said below
- ln1_gain: bfloat16 [2048], P('dp'), may hold values from 0.5 to 1.5
- ln1_bias: bfloat16 [2048], P('dp'), may hold values from -4 to 4
- qkv_weight: bfloat16 [2048, 3, 2048], P('dp', None, 'tensor'), may hold values from -0.125 to 0.125
- qv_bias: bfloat16 [2, 16, 128], P(None, 'tensor', 'dp'), may hold values from -4 to 4
- out_weight: bfloat16 [2048, 2048], P('tensor', 'dp'), may hold values from -0.75 to 0.75
- out_bias: bfloat16 [2048], P('dp'), may hold values from -4 to 4
- ln2_gain: bfloat16 [2048], P('dp'), may hold values from 0.5 to 1.5
- ln2_bias: bfloat16 [2048], P('dp'), may hold values from -4 to 4
- up_weight: bfloat16 [2048, 8192], P('dp', 'tensor'), may hold values from -0.125 to 0.125
- up_bias: bfloat16 [512, 16], P('tensor', 'dp'), may hold values from -4 to 4
- down_weight: bfloat16 [8192, 2048], P('tensor', 'dp'), may hold values from -0.0625 to 0.0625
- down_bias: bfloat16 [2048], P('dp'), may hold values from -4 to 4
- cotangent: bfloat16 [8192, 2048], P(('dp', 'tensor')), may hold values from -6 to 6
Outputs:
- output: bfloat16 [8192, 2048], P(('dp', 'tensor'))
- tokens_grad: float32 [8192, 2048], P(('dp', 'tensor'))
- ln1_gain_grad: float32 [2048], P('dp')
- ln1_bias_grad: float32 [2048], P('dp')
- qkv_weight_grad: float32 [2048, 3, 2048], P('dp', None, 'tensor')
- qv_bias_grad: float32 [2, 16, 128], P(None, 'tensor', 'dp')
- out_weight_grad: float32 [2048, 2048], P('tensor', 'dp')
- out_bias_grad: float32 [2048], P('dp')
- ln2_gain_grad: float32 [2048], P('dp')
- ln2_bias_grad: float32 [2048], P('dp')
- up_weight_grad: float32 [2048, 8192], P('dp', 'tensor')
- up_bias_grad: float32 [512, 16], P('tensor', 'dp')
- down_weight_grad: float32 [8192, 2048], P('tensor', 'dp')
- down_bias_grad: float32 [2048], P('dp')
- stream_rms: float32 [5], replicated
Inputs may be any that keep to these rules, and one draw needn't show every extreme that they name: `lengths`: each sequence's true token count.
All inputs are finite; a program needn't handle non-finite values.
Results may differ from a plain program's by a relative error of at most 0.02.
Values may be sent and summed in bfloat16 or wider, within the bound.
A program may use at most 256 MiB of HBM per device.

v0:
```python
import jax
import jax.numpy as jnp
from jax import lax
from jax.sharding import PartitionSpec as P

D = 2048
HD = 128
LEN = 1024
EPS = 1e-05


def layer_norm(values, norm_gain, norm_shift):
    center = values - jnp.mean(values, axis=-1, keepdims=True)
    spread = lax.rsqrt(jnp.mean(center * center, axis=-1, keepdims=True) + EPS)
    normed = center * spread
    return (normed * norm_gain + norm_shift, normed, spread)


def norm_backward(upstream, normed, spread, norm_gain):
    scaled = upstream * norm_gain
    mean_part = jnp.mean(scaled, axis=-1, keepdims=True)
    across = jnp.mean(scaled * normed, axis=-1, keepdims=True)
    return spread * (scaled - mean_part - normed * across)


def gelu_tanh(values):
    return jax.nn.gelu(values, approximate=True)


def contract_rows(left, right):
    return lax.dot_general(
        left, right, (((0,), (0,)), ((), ())), preferred_element_type=jnp.float32
    )


def contract_cols(left, right):
    return lax.dot_general(
        left, right, (((1,), (1,)), ((), ())), preferred_element_type=jnp.float32
    )


def allowed_keys(first_row, block_size, positions, length):
    query_pos = first_row + jnp.arange(block_size, dtype=jnp.int32)
    return (positions[None, :] <= query_pos[:, None]) & (positions[None, :] < length)


def attend_forward(queries, key_rows, value_rows, length):
    block_size = min(512, LEN)
    positions = jnp.arange(LEN, dtype=jnp.int32)
    score_scale = HD ** (-0.5)

    def one_block(block_index):
        first_row = block_index * block_size
        query_block = lax.dynamic_slice_in_dim(queries, first_row, block_size, 0)
        scores = (
            jnp.einsum("qhd,khd->hqk", query_block, key_rows, preferred_element_type=jnp.float32)
            * score_scale
        )
        allowed = allowed_keys(first_row, block_size, positions, length)
        scores = jnp.where(allowed[None], scores, -1e30)
        row_max = jnp.max(scores, axis=-1, keepdims=True)
        powers = jnp.exp(scores - row_max)
        totals = jnp.sum(powers, axis=-1, keepdims=True)
        shares = (powers / totals).astype(jnp.bfloat16)
        mixed = jnp.einsum("hqk,khd->qhd", shares, value_rows, preferred_element_type=jnp.float32)
        return (mixed.astype(jnp.bfloat16), (row_max + jnp.log(totals))[..., 0])

    mixed, log_totals = lax.map(one_block, jnp.arange(LEN // block_size, dtype=jnp.int32))
    return (mixed.reshape(LEN, queries.shape[1], HD), log_totals)


def attend_backward(queries, key_rows, value_rows, grad_out, log_totals, length):
    block_size = min(512, LEN)
    positions = jnp.arange(LEN, dtype=jnp.int32)
    score_scale = HD ** (-0.5)

    def one_block(carry, block_index):
        key_grad, value_grad = carry
        first_row = block_index * block_size
        query_block = lax.dynamic_slice_in_dim(queries, first_row, block_size, 0)
        grad_block = lax.dynamic_slice_in_dim(grad_out, first_row, block_size, 0)
        scores = (
            jnp.einsum("qhd,khd->hqk", query_block, key_rows, preferred_element_type=jnp.float32)
            * score_scale
        )
        allowed = allowed_keys(first_row, block_size, positions, length)
        shares = jnp.where(allowed[None], jnp.exp(scores - log_totals[block_index][..., None]), 0.0)
        value_grad = value_grad + jnp.einsum(
            "hqk,qhd->khd",
            shares.astype(jnp.bfloat16),
            grad_block,
            preferred_element_type=jnp.float32,
        )
        share_grad = jnp.einsum(
            "qhd,khd->hqk", grad_block, value_rows, preferred_element_type=jnp.float32
        )
        centre = jnp.sum(shares * share_grad, axis=-1, keepdims=True)
        score_grad = (shares * (share_grad - centre)).astype(jnp.bfloat16)
        query_grad = (
            jnp.einsum("hqk,khd->qhd", score_grad, key_rows, preferred_element_type=jnp.float32)
            * score_scale
        )
        key_grad = (
            key_grad
            + jnp.einsum(
                "hqk,qhd->khd", score_grad, query_block, preferred_element_type=jnp.float32
            )
            * score_scale
        )
        return ((key_grad, value_grad), query_grad.astype(jnp.bfloat16))

    zeros_kv = jnp.zeros((LEN, queries.shape[1], HD), jnp.float32)
    (key_grad, value_grad), query_grads = lax.scan(
        one_block, (zeros_kv, zeros_kv), jnp.arange(LEN // block_size, dtype=jnp.int32)
    )
    return (
        query_grads.reshape(LEN, queries.shape[1], HD),
        key_grad.astype(jnp.bfloat16),
        value_grad.astype(jnp.bfloat16),
    )


def shards(
    tokens,
    lengths,
    ln1_gain,
    ln1_bias,
    qkv_weight,
    qv_bias,
    out_weight,
    out_bias,
    ln2_gain,
    ln2_bias,
    up_weight,
    up_bias,
    down_weight,
    down_bias,
    cotangent,
):
    (
        gain_one,
        shift_one,
        qkv_full,
        qv_full,
        out_full,
        out_shift,
        gain_two,
        shift_two,
        up_full,
        up_shift,
        down_full,
        down_shift,
    ) = (
        lax.all_gather(ln1_gain, "dp", axis=0, tiled=True),
        lax.all_gather(ln1_bias, "dp", axis=0, tiled=True),
        lax.all_gather(qkv_weight, "dp", axis=0, tiled=True),
        lax.all_gather(qv_bias, "dp", axis=2, tiled=True),
        lax.all_gather(out_weight, "dp", axis=1, tiled=True),
        lax.all_gather(out_bias, "dp", axis=0, tiled=True),
        lax.all_gather(ln2_gain, "dp", axis=0, tiled=True),
        lax.all_gather(ln2_bias, "dp", axis=0, tiled=True),
        lax.all_gather(up_weight, "dp", axis=0, tiled=True),
        lax.all_gather(up_bias, "dp", axis=1, tiled=True),
        lax.all_gather(down_weight, "dp", axis=1, tiled=True),
        lax.all_gather(down_bias, "dp", axis=0, tiled=True),
    )
    gain_one = gain_one.astype(jnp.float32)
    shift_one = shift_one.astype(jnp.float32)
    gain_two = gain_two.astype(jnp.float32)
    shift_two = shift_two.astype(jnp.float32)
    out_shift = out_shift.astype(jnp.float32)
    down_shift = down_shift.astype(jnp.float32)
    own_rows = tokens.shape[0]
    group_rows = own_rows * lax.axis_size("tensor")
    seq_count = lengths.shape[0]
    local_heads = qkv_full.shape[2] // HD
    local_width = qkv_full.shape[2]
    local_hidden = up_full.shape[1]
    own_first = lax.axis_index("tensor") * own_rows
    positions = jnp.arange(group_rows, dtype=jnp.int32)
    seq_ids = positions // LEN
    length_rows = jnp.sum(
        jnp.where(
            seq_ids[:, None] == jnp.arange(seq_count, dtype=jnp.int32)[None, :], lengths[None, :], 0
        ),
        axis=1,
    )
    valid_all = (positions % LEN < length_rows).astype(jnp.float32)[:, None]
    valid_own = lax.dynamic_slice_in_dim(valid_all, own_first, own_rows, 0)
    own_count = jnp.sum(valid_own)
    tokens_in, cotangent_in = (
        lax.all_gather(tokens, "tensor", axis=0, tiled=True),
        lax.all_gather(cotangent, "tensor", axis=0, tiled=True),
    )

    def own_part(values):
        return lax.dynamic_slice_in_dim(values, own_first, own_rows, 0)

    def branch_total(source, weight):
        return lax.psum(
            jnp.dot(source, weight, preferred_element_type=jnp.float32).astype(jnp.bfloat16),
            "tensor",
        ).astype(jnp.float32)

    def input_total(source, weight):
        return lax.psum(contract_cols(source, weight).astype(jnp.bfloat16), "tensor").astype(
            jnp.float32
        )

    recorded = []

    def record(values):
        mine = own_part(values)
        square_sum = jnp.sum(valid_own * mine * mine)
        recorded.append(lax.psum((square_sum, own_count), ("dp", "tensor")))

    x_values = tokens_in.astype(jnp.float32)
    record(x_values)
    ln1_out, normed_one, spread_one = layer_norm(x_values, gain_one, shift_one)
    normed_a = ln1_out.astype(jnp.bfloat16)
    qkv_flat = qkv_full.reshape(D, 3 * local_width)
    projected = jnp.dot(normed_a, qkv_flat, preferred_element_type=jnp.float32)
    qv_values = qv_full.astype(jnp.float32)
    bias_all = jnp.stack([qv_values[0], jnp.zeros_like(qv_values[0]), qv_values[1]]).reshape(
        3 * local_width
    )
    qkv_low = (projected + bias_all).astype(jnp.bfloat16)
    qkv_seq = qkv_low.reshape(seq_count, LEN, 3, local_heads, HD)

    def forward_sequence(pair):
        seq_qkv, seq_len = pair
        return attend_forward(seq_qkv[:, 0], seq_qkv[:, 1], seq_qkv[:, 2], seq_len)

    attended, log_totals = lax.map(forward_sequence, (qkv_seq, lengths))
    attended_rows = attended.reshape(group_rows, local_width)
    attn_out = branch_total(attended_rows, out_full) + out_shift
    record(attn_out)
    middle = x_values + attn_out
    record(middle)
    ln2_out, normed_two, spread_two = layer_norm(middle, gain_two, shift_two)
    normed_c = ln2_out.astype(jnp.bfloat16)
    hidden_pre = jnp.dot(normed_c, up_full, preferred_element_type=jnp.float32) + up_shift.astype(
        jnp.float32
    ).reshape(local_hidden)
    hidden_act = gelu_tanh(hidden_pre).astype(jnp.bfloat16)
    mlp_out = branch_total(hidden_act, down_full) + down_shift
    record(mlp_out)
    result = middle + mlp_out
    record(result)
    grad_y = cotangent_in.astype(jnp.float32) * valid_all
    down_bias_grad = jnp.sum(own_part(grad_y), axis=0)
    grad_m = grad_y.astype(jnp.bfloat16)
    down_weight_grad = contract_rows(hidden_act, grad_m)
    grad_act = contract_cols(grad_m, down_full)
    gelu_value, gelu_back = jax.vjp(gelu_tanh, hidden_pre)
    grad_u = gelu_back(grad_act)[0].astype(jnp.bfloat16)
    up_bias_grad = jnp.sum(grad_u, axis=0, dtype=jnp.float32).reshape(local_hidden // 16, 16)
    up_weight_grad = contract_rows(normed_c, grad_u)
    grad_c = input_total(grad_u, up_full)
    grad_mid = grad_y + norm_backward(grad_c, normed_two, spread_two, gain_two)
    ln2_gain_grad = jnp.sum(own_part(grad_c * normed_two), axis=0)
    ln2_bias_grad = jnp.sum(own_part(grad_c), axis=0)
    out_bias_grad = jnp.sum(own_part(grad_mid), axis=0)
    grad_z = grad_mid.astype(jnp.bfloat16)
    out_weight_grad = contract_rows(attended_rows, grad_z)
    grad_o = contract_cols(grad_z, out_full).astype(jnp.bfloat16)
    grad_o_seq = grad_o.reshape(seq_count, LEN, local_heads, HD)

    def backward_sequence(group):
        seq_qkv, seq_grad, seq_totals, seq_len = group
        return attend_backward(
            seq_qkv[:, 0], seq_qkv[:, 1], seq_qkv[:, 2], seq_grad, seq_totals, seq_len
        )

    grad_q, grad_k, grad_v = lax.map(backward_sequence, (qkv_seq, grad_o_seq, log_totals, lengths))
    grad_qkv = jnp.stack([grad_q, grad_k, grad_v], axis=2).reshape(group_rows, 3 * local_width)
    qv_bias_grad = jnp.stack(
        [
            jnp.sum(grad_q, axis=(0, 1), dtype=jnp.float32),
            jnp.sum(grad_v, axis=(0, 1), dtype=jnp.float32),
        ]
    )
    qkv_weight_grad = contract_rows(normed_a, grad_qkv).reshape(D, 3, local_width)
    grad_a = input_total(grad_qkv, qkv_flat)
    grad_x_all = grad_mid + norm_backward(grad_a, normed_one, spread_one, gain_one)
    tokens_grad = own_part(grad_x_all)
    ln1_gain_grad = jnp.sum(own_part(grad_a * normed_one), axis=0)
    ln1_bias_grad = jnp.sum(own_part(grad_a), axis=0)
    (
        qkv_weight_out,
        qv_bias_out,
        out_weight_out,
        up_weight_out,
        up_bias_out,
        down_weight_out,
        ln1_gain_part,
        ln1_bias_part,
        out_bias_part,
        ln2_gain_part,
        ln2_bias_part,
        down_bias_part,
    ) = (
        lax.psum_scatter(
            qkv_weight_grad.astype(jnp.bfloat16), "dp", scatter_dimension=0, tiled=True
        ).astype(jnp.float32),
        lax.psum_scatter(
            qv_bias_grad.astype(jnp.bfloat16), "dp", scatter_dimension=2, tiled=True
        ).astype(jnp.float32),
        lax.psum_scatter(
            out_weight_grad.astype(jnp.bfloat16), "dp", scatter_dimension=1, tiled=True
        ).astype(jnp.float32),
        lax.psum_scatter(
            up_weight_grad.astype(jnp.bfloat16), "dp", scatter_dimension=0, tiled=True
        ).astype(jnp.float32),
        lax.psum_scatter(
            up_bias_grad.astype(jnp.bfloat16), "dp", scatter_dimension=1, tiled=True
        ).astype(jnp.float32),
        lax.psum_scatter(
            down_weight_grad.astype(jnp.bfloat16), "dp", scatter_dimension=1, tiled=True
        ).astype(jnp.float32),
        lax.psum_scatter(
            ln1_gain_grad.astype(jnp.bfloat16), "dp", scatter_dimension=0, tiled=True
        ).astype(jnp.float32),
        lax.psum_scatter(
            ln1_bias_grad.astype(jnp.bfloat16), "dp", scatter_dimension=0, tiled=True
        ).astype(jnp.float32),
        lax.psum_scatter(
            out_bias_grad.astype(jnp.bfloat16), "dp", scatter_dimension=0, tiled=True
        ).astype(jnp.float32),
        lax.psum_scatter(
            ln2_gain_grad.astype(jnp.bfloat16), "dp", scatter_dimension=0, tiled=True
        ).astype(jnp.float32),
        lax.psum_scatter(
            ln2_bias_grad.astype(jnp.bfloat16), "dp", scatter_dimension=0, tiled=True
        ).astype(jnp.float32),
        lax.psum_scatter(
            down_bias_grad.astype(jnp.bfloat16), "dp", scatter_dimension=0, tiled=True
        ).astype(jnp.float32),
    )
    ln1_gain_out, ln1_bias_out, out_bias_out, ln2_gain_out, ln2_bias_out, down_bias_out = lax.psum(
        (ln1_gain_part, ln1_bias_part, out_bias_part, ln2_gain_part, ln2_bias_part, down_bias_part),
        "tensor",
    )
    totals = jnp.stack([entry[0] for entry in recorded])
    count = recorded[0][1]
    stream_rms = jnp.sqrt(totals / (count * D))
    return (
        own_part(result).astype(jnp.bfloat16),
        tokens_grad,
        ln1_gain_out,
        ln1_bias_out,
        qkv_weight_out,
        qv_bias_out,
        out_weight_out,
        out_bias_out,
        ln2_gain_out,
        ln2_bias_out,
        up_weight_out,
        up_bias_out,
        down_weight_out,
        down_bias_out,
        stream_rms,
    )


def solution(mesh):
    placed = (
        P(("dp", "tensor"), None),
        P("dp"),
        P("dp"),
        P("dp"),
        P("dp", None, "tensor"),
        P(None, "tensor", "dp"),
        P("tensor", "dp"),
        P("dp"),
        P("dp"),
        P("dp"),
        P("dp", "tensor"),
        P("tensor", "dp"),
        P("tensor", "dp"),
        P("dp"),
        P(("dp", "tensor"), None),
    )
    return jax.shard_map(
        shards,
        mesh=mesh,
        in_specs=placed,
        out_specs=(
            P(("dp", "tensor"), None),
            P(("dp", "tensor"), None),
            P("dp"),
            P("dp"),
            P("dp", None, "tensor"),
            P(None, "tensor", "dp"),
            P("tensor", "dp"),
            P("dp"),
            P("dp"),
            P("dp"),
            P("dp", "tensor"),
            P("tensor", "dp"),
            P("tensor", "dp"),
            P("dp"),
            P(),
        ),
        check_vma=False,
    )
```

profile of v0, /device:TPU:0, one launch (start us, length us, event | category | flops | bytes accessed | tf_op | source)
XLA Modules:
  0.0 1390.4 jit_solution(11187329936646952826)
XLA Ops:
  12.4 10.4 all-gather.1
  22.8 8.9 all-gather
  32.5 8.3 all_gather.46
  41.2 51.9 %all-gather.14.cloned.1.call-done = bf16[1024,2048]{1,0:T(8,128)(2,1)} async-done(((bf16[256,2048]{1,0:T(8,128)(2,1)}), bf16[1024,2048]{1,0:T(8,128)(2,1)}) %all-gather.14.cloned.1.call-update) | async-done | bytes 4194320 | tf_op jit(solution)/shard_map/all_gather | solution.py:192
  99.3 41.3 %all-gather.16.cloned.1.call-done = bf16[2048,3,512]{0,2,1:T(8,128)(2,1)} async-done(((bf16[256,3,512]{0,2,1:T(8,128)(2,1)}), bf16[2048,3,512]{0,2,1:T(8,128)(2,1)}) %all-gather.16.cloned.1.call-update) | async-done | bytes 6291472 | tf_op jit(solution)/shard_map/all_gather | solution.py:156
  140.6 12.5 add_convert_fusion.2
  153.1 6.3 squeeze.48
  162.8 22.4 %while.50 = (s32[]{:T(128)}, bf16[2,512,4,128]{3,2,1,0:T(4,128)(2,1)}, f32[2,4,512]{2,1,0:T(4,128)S(1)}, s32[2]{0:T(128)S(1)}, s32[]{:T(128)}, /*index=5*/bf16[1...) while((s32[]{:T(128)}, ...), condition=%wide.region_5.6_spmd.clone.clone, body=%wide.region_2.5_spmd.clone.clone.sunk | while | flops 1100217856 | bytes 39917828 | solution.py:68
  185.3 7.0 convolution_convert_fusion.6
  195.1 8.8 all-gather.4
  203.9 8.1 all-gather.3
  212.0 8.8 all-gather.2
  220.8 8.0 all-gather.5
  229.0 118.4 %all-reduce.15.cloned.1.call-done = bf16[1024,2048]{1,0:T(8,128)(2,1)} async-done(((bf16[1024,2048]{1,0:T(8,128)(2,1)}), bf16[1024,2048]{1,0:T(8,128)(2,1)}) %all-reduce.15.cloned.1.call-update) | async-done | bytes 4194320 | tf_op jit(solution)/shard_map/psum | solution.py:200
  347.4 11.2 fusion.84
  358.6 4.5 multiply_reduce_fusion.3
  368.3 34.0 %all-gather.20.cloned.1.call-done = bf16[2048,2048]{1,0:T(8,128)(2,1)} async-done(((bf16[256,2048]{1,0:T(8,128)(2,1)}), bf16[2048,2048]{1,0:T(8,128)(2,1)}) %all-gather.20.cloned.1.call-update) | async-done | bytes 8388624 | tf_op jit(solution)/shard_map/all_gather | solution.py:162
  402.4 15.9 %fusion.69 = f32[1024,2048]{1,0:T(8,128)} fusion(bf16[2048,2048]{1,0:T(8,128)(2,1)} %all-gather.20.cloned.1.call-done, f32[1024,2048]{1,0:T(8,128)} %subtract_multiply_fusion, f32[2048]{0:T(1024)S(1)} %bitcast.153, f32[2048]{0:T(1024)S(1)} %bitcast.140), kind=kOutput, calls=%fused_computation.120 | convolution fusion | flops 8596226048 | bytes 25182208 | tf_op jit(solution)/shard_map/dot_general | solution.py:242
  418.3 66.3 %all-gather.24.cloned.1.call-done = bf16[1024,2048]{1,0:T(8,128)(2,1)} async-done(((bf16[256,2048]{1,0:T(8,128)(2,1)}), bf16[1024,2048]{1,0:T(8,128)(2,1)}) %all-gather.24.cloned.1.call-update) | async-done | bytes 4194320 | tf_op jit(solution)/shard_map/all_gather | solution.py:193
  484.6 56.3 %all-gather.22.cloned.1.call-done = bf16[2048,2048]{1,0:T(8,128)(2,1)} async-done(((bf16[2048,256]{1,0:T(8,128)(2,1)}), bf16[2048,2048]{1,0:T(8,128)(2,1)}) %all-gather.22.cloned.1.call-update) | async-done | bytes 8388624 | tf_op jit(solution)/shard_map/all_gather | solution.py:164
  540.8 19.2 %fusion.87 = (bf16[2048]{0:T(1024)(128)(2,1)}, bf16[1024,2048]{1,0:T(8,128)(2,1)S(1)}) fusion(f32[1024,2048]{1,0:T(8,128)} %fusion.69, f32[2048]{0:T(1024)S(1)} %reshape.277, bf16[2048,2048]{1,0:T(8,128)(2,1)} %all-gather.22.cloned.1.call-done, f32[1024]{0:T(1024)S(1)} %fusion.82, bf16[1024,2048]{1,0:T(8,128)(2,1)} %all-gather.24.cloned.1.call-done), kind=kOutput, calls=%fused_computation.167 | convolution fusion | flops 8642361344 | bytes 25182208 | tf_op jit(solution)/shard_map/dot_general | solution.py:37
  562.1 13.1 convolution_convert_fusion.4
  575.3 155.1 %all-reduce.17.cloned.1.call-done = bf16[1024,2048]{1,0:T(8,128)(2,1)} async-done(((bf16[1024,2048]{1,0:T(8,128)(2,1)}), bf16[1024,2048]{1,0:T(8,128)(2,1)}) %all-reduce.17.cloned.1.call-update) | async-done | bytes 4194320 | tf_op jit(solution)/shard_map/psum | solution.py:206
  730.4 6.0 multiply_reduce_fusion.5
  737.5 8.4 convert_multiply_fusion
  745.8 6.5 fusion.66
  752.4 41.1 %while.51 = (s32[]{:T(128)}, f32[1024,4,128]{0,2,1:T(8,128)S(1)}, f32[1024,4,128]{0,2,1:T(8,128)}, bf16[2,512,4,128]{3,1,2,0:T(8,128)(2,1)}, s32[2]{0:T(128)S(1)...) while((s32[]{:T(128)}, f32[1024,4,128]{0,2,1:T(8,128)S(1)}, ...), condition=%wide.region_15.16_spmd.clone.clone, body=%wide.region_13.15_spmd.clone.clone.sunk | while | flops 2720005632 | bytes 100202928 | solution.py:113
  763.0 4.0 multiply_reduce_fusion.8
  779.1 5.1 bitcast_add_fusion.5
  784.2 4.0 multiply_reduce_fusion.8
  797.8 7.4 convolution_convert_fusion.7
  805.3 16.3 %convolution_convert_fusion.5 = bf16[1024,2048]{1,0:T(8,128)(2,1)} fusion(bf16[2048,2048]{1,0:T(8,128)(2,1)} %all-gather.22.cloned.1.call-done, f32[1024,2048]{1,0:T(8,128)} %fusion.69, f32[2048]{0:T(1024)S(1)} %copy-done.27), kind=kOutput, calls=%fused_computation.86 | convolution fusion | flops 8613003264 | bytes 20979712 | tf_op jit(solution)/shard_map/dot_general | solution.py:201
  827.6 4.7 copy.114
  832.3 11.2 convolution_convert_fusion.3
  844.2 20.2 %convolution_convert_fusion = bf16[2048,2048]{1,0:T(8,128)(2,1)} fusion(bf16[1024,2048]{1,0:T(8,128)(2,1)} %all-gather.24.cloned.1.call-done, f32[1024]{0:T(1024)S(1)} %copy-done.25, f32[1024,2048]{1,0:T(8,128)} %fusion.69, f32[2048]{0:T(1024)S(1)} %copy-done.27), kind=kOutput, calls=%fused_computation.77 | convolution fusion | flops 8621391872 | bytes 20983808 | tf_op jit(solution)/shard_map/dot_general | solution.py:31
  865.1 14.8 %convolution_convert_fusion.1 = bf16[2048,2048]{1,0:T(8,128)(2,1)} fusion(bf16[1024,2048]{1,0:T(8,128)(2,1)} %copy-done.39, f32[1024,2048]{1,0:T(8,128)} %subtract_multiply_fusion, f32[2048]{0:T(1024)S(1)} %bitcast.154, f32[2048]{0:T(1024)S(1)} %bitcast.143), kind=kOutput, calls=%fused_computation.78 | convolution fusion | flops 8600420352 | bytes 20987904 | tf_op jit(solution)/shard_map/dot_general | solution.py:31
  880.6 14.2 %convolution_convert_fusion.2 = bf16[2048,3,512]{2,0,1:T(8,128)(2,1)} fusion(bf16[3,512,1024]{2,1,0:T(8,128)(2,1)} %bitcast.135, f32[2048]{0:T(1024)S(1)} %bitcast.152, f32[2048]{0:T(1024)S(1)} %bitcast.145, bf16[1024,2048]{1,0:T(8,128)(2,1)} %all-gather.14.cloned.1.call-done, f32[1024]{0:T(1024)S(1)} %copy-done.23, f32[1024]{0:T(1024)S(1)} %copy-done.19), kind=kOutput, calls=%fused_computation.81 | convolution fusion | flops 6458179584 | bytes 13656064 | tf_op jit(solution)/shard_map/dot_general | solution.py:31
  896.7 9.1 all-gather.6
  906.6 6.5 convert_element_type.197
  923.4 243.2 %all-reduce.19.cloned.1.call-done = (bf16[1024,2048]{1,0:T(8,128)(2,1)}, bf16[1024,2048]{1,0:T(8,128)(2,1)}) async-done(((bf16[1024,2048]{1,0:T(8,128)(2,1)}, bf16[1024,2048]{1,0:T(8,128)(2,1)}), (bf16[1024,2048]{1,0:T(8,128)(2,1)}, bf16[1024,2048]{1,0:T(8,128)(2,1)})) %all-reduce.19.cloned.1.call-update) | async-done | bytes 8388624 | tf_op jit(solution)/shard_map/psum | solution.py:200
  1170.0 5.6 fusion.52
  1175.6 40.5 %all-reduce.7 = (f32[1]{0:T(128)}, f32[1]{0:T(128)}, f32[1]{0:T(128)}, f32[1]{0:T(128)}, f32[1]{0:T(128)}, /*index=5*/f32[]{:T(128)}) all-reduce(f32[1]{0:T(128)} %bitcast.25, f32[1]{0:T(128)} %bitcast.26, f32[1]{0:T(128)} %bitcast.27, f32[1]{0:T(128)} %bitcast.28, ...), channel_id=1, replica_groups=mesh['dp'=8,'tensor'=4] {'dp','tensor'}, use_global_device_ids=true, to_apply=%region_47.48 | all-reduce | flops 6 | bytes 48 | tf_op jit(solution)/shard_map/psum | solution.py:215
  1216.1 6.7 convert_element_type.225
  1225.8 4.8 dynamic-slice_reduce_fusion.3
  1230.6 24.5 %all-reduce.9 = (bf16[2048]{0:T(1024)(128)(2,1)S(1)}, bf16[2048]{0:T(1024)(128)(2,1)S(1)}, bf16[2048]{0:T(1024)(128)(2,1)S(1)}, bf16[2048]{0:T(1024)(128)(2,1)S(...) all-reduce(bf16[2048]{0:T(1024)(128)(2,1)S(1)} %get-tuple-element.5, ...), channel_id=2, replica_groups=mesh['dp'=8,'tensor'=4] {'dp'}, use_global_device_ids=true, to_apply=%region_20.21.clone | all-reduce | flops 14336 | bytes 57344
  1262.7 53.5 %reduce-scatter.13.cloned.1.call-done = bf16[256,2048]{1,0:T(8,128)(2,1)} async-done(((bf16[2048,2048]{1,0:T(8,128)(2,1)}), bf16[256,2048]{1,0:T(8,128)(2,1)}) %reduce-scatter.13.cloned.1.call-update) | async-done | bytes 1048592 | tf_op jit(solution)/shard_map/reduce_scatter | solution.py:312
  1319.5 12.5 all-reduce.8
  1332.5 48.7 %reduce-scatter.9.cloned.1.call-done = bf16[256,3,512]{2,0,1:T(8,128)(2,1)} async-done(((bf16[2048,3,512]{2,0,1:T(8,128)(2,1)}), bf16[256,3,512]{2,0,1:T(8,128)(2,1)}) %reduce-scatter.9.cloned.1.call-update) | async-done | bytes 786448 | tf_op jit(solution)/shard_map/reduce_scatter | solution.py:303
  (244 shorter events, 113.4 us)
Async XLA Ops:
  7.2 85.9 %all-gather.14.cloned.1.call-start = ((), (), s32[]{:S(2)}) async-start(), calls=%async_computation.5 | async-start | bytes 5242880 | tf_op jit(solution)/shard_map/all_gather | solution.py:192
  7.9 132.7 %all-gather.16.cloned.1.call-start = ((), (), s32[]{:S(2)}) async-start(), calls=%async_computation.6 | async-start | bytes 7077888 | tf_op jit(solution)/shard_map/all_gather | solution.py:156
  10.3 175.0 %all-gather.18.cloned.1.call-start = ((), (), s32[]{:S(2)}) async-start(), calls=%async_computation.7 | async-start | bytes 2359296 | tf_op jit(solution)/shard_map/all_gather | solution.py:158
  11.0 336.4 %all-reduce.15.cloned.1.call-start = ((), (), s32[]{:S(2)}) async-start(), calls=%async_computation.8 | async-start | bytes 8388608 | tf_op jit(solution)/shard_map/psum | solution.py:200
  22.8 130.3 %copy-start.28 = (f32[8,1,256]{2,1,0:T(1,128)}, f32[8,1,256]{2,1,0:T(1,128)S(1)}, u32[]{:S(2)}) copy-start(f32[8,1,256]{2,1,0:T(1,128)S(1)} %convert_element_type.259) | copy-start | bytes 24580
  31.7 121.3 %copy-start.20 = (f32[8,1,256]{2,1,0:T(1,128)}, f32[8,1,256]{2,1,0:T(1,128)S(1)}, u32[]{:S(2)}) copy-start(f32[8,1,256]{2,1,0:T(1,128)S(1)} %convert_element_type.258) | copy-start | bytes 24580
  95.9 57.2 %copy-start.18 = (f32[1024]{0:T(1024)}, f32[1024]{0:T(1024)S(1)}, u32[]{:S(2)}) copy-start(f32[1024]{0:T(1024)S(1)} %broadcast_multiply_fusion.6) | copy-start | bytes 12292
  99.3 53.8 %copy-start.22 = (f32[1024]{0:T(1024)}, f32[1024]{0:T(1024)S(1)}, u32[]{:S(2)}) copy-start(f32[1024]{0:T(1024)S(1)} %add_rsqrt_fusion.1) | copy-start | bytes 12292
  169.3 3.2 copy-start.14
  180.4 3.2 copy-start.14
  185.2 7.7 copy-start.2
  185.2 7.7 copy-start.6
  185.3 9.7 copy-start.34
  185.3 9.7 copy-start.35
  185.3 9.7 copy-start.36
  185.3 35.5 %copy-start.33 = (bf16[128,2]{0,1:T(2,128)(2,1)S(1)}, bf16[128,2]{0,1:T(2,128)(2,1)}, u32[]{:S(2)}) copy-start(bf16[128,2]{0,1:T(2,128)(2,1)} %param.30) | copy-start | bytes 1540
  192.4 210.0 %all-gather.20.cloned.1.call-start = ((), (), s32[]{:S(2)}) async-start(), calls=%async_computation.9 | async-start | bytes 9437184 | tf_op jit(solution)/shard_map/all_gather | solution.py:162
  193.0 291.6 %all-gather.24.cloned.1.call-start = ((), (), s32[]{:S(2)}) async-start(), calls=%async_computation.11 | async-start | bytes 5242880 | tf_op jit(solution)/shard_map/all_gather | solution.py:193
  193.6 347.3 %all-gather.22.cloned.1.call-start = ((), (), s32[]{:S(2)}) async-start(), calls=%async_computation.10 | async-start | bytes 9437184 | tf_op jit(solution)/shard_map/all_gather | solution.py:164
  194.3 536.0 %all-reduce.17.cloned.1.call-start = ((), (), s32[]{:S(2)}) async-start(), calls=%async_computation.12 | async-start | bytes 8388608 | tf_op jit(solution)/shard_map/psum | solution.py:206
  203.9 198.5 %copy-start.30 = (f32[8,1,256]{2,1,0:T(1,128)}, f32[8,1,256]{2,1,0:T(1,128)S(1)}, u32[]{:S(2)}) copy-start(f32[8,1,256]{2,1,0:T(1,128)S(1)} %convert_element_type.262) | copy-start | bytes 24580
  212.0 524.4 %copy-start.16 = (f32[8,1,256]{2,1,0:T(1,128)}, f32[8,1,256]{2,1,0:T(1,128)S(1)}, u32[]{:S(2)}) copy-start(f32[8,1,256]{2,1,0:T(1,128)S(1)} %convert_element_type.261) | copy-start | bytes 24580
  228.9 311.9 %copy-start.26 = (f32[2048]{0:T(1024)}, f32[2048]{0:T(1024)S(1)}, u32[]{:S(2)}) copy-start(f32[2048]{0:T(1024)S(1)} %reshape.277) | copy-start | bytes 24580
  229.0 507.4 %copy-start.24 = (f32[1024]{0:T(1024)}, f32[1024]{0:T(1024)S(1)}, u32[]{:S(2)}) copy-start(f32[1024]{0:T(1024)S(1)} %fusion.82) | copy-start | bytes 12292
  358.6 5.8 copy-start
  575.2 344.9 %reduce-scatter.17.cloned.1.call-start = ((), (), s32[]{:S(2)}) async-start(), calls=%async_computation.17 | async-start | bytes 36864
  730.4 6.0 copy-start.5
  730.4 7.1 copy-start.10
  745.8 6.5 copy-start.4
  755.7 3.5 copy-start.9
  759.2 3.8 copy-start.7
  767.1 2.5 copy-start.11
  767.1 3.9 copy-start.3
  775.5 3.5 copy-start.9
  779.1 5.1 copy-start.7
  788.2 3.9 copy-start.3
  795.3 10.0 copy-start.27
  797.8 123.8 %reduce-scatter.11.cloned.1.call-start = ((), (), s32[]{:S(2)}) async-start(), calls=%async_computation.14 | async-start | bytes 2359296 | tf_op jit(solution)/shard_map/reduce_scatter | solution.py:309
  805.3 361.3 %all-reduce.19.cloned.1.call-start = ((), (), s32[]{:S(2)}) async-start(), calls=%async_computation.18 | async-start | bytes 16777216 | tf_op jit(solution)/shard_map/psum | solution.py:200
  805.3 16.4 %copy-start.13 = (bf16[2,512,4,128]{3,1,2,0:T(8,128)(2,1)S(1)}, bf16[2,512,4,128]{3,1,2,0:T(8,128)(2,1)}, u32[]{:S(2)}) copy-start(bf16[2,512,4,128]{3,1,2,0:T(8,128)(2,1)} %get-tuple-element.174) | copy-start | bytes 3145732
  843.5 416.4 %reduce-scatter.15.cloned.1.call-start = ((), (), s32[]{:S(2)}) async-start(), calls=%async_computation.16 | async-start | bytes 9437184 | tf_op jit(solution)/shard_map/reduce_scatter | solution.py:318
  864.4 451.8 %reduce-scatter.13.cloned.1.call-start = ((), (), s32[]{:S(2)}) async-start(), calls=%async_computation.15 | async-start | bytes 9437184 | tf_op jit(solution)/shard_map/reduce_scatter | solution.py:312
  880.0 501.2 %reduce-scatter.9.cloned.1.call-start = ((), (), s32[]{:S(2)}) async-start(), calls=%async_computation.13 | async-start | bytes 7077888 | tf_op jit(solution)/shard_map/reduce_scatter | solution.py:303
  880.6 14.2 %copy-start.38 = (u32[32]{0:T(128)S(1)}, u32[32]{0:T(128)}, u32[]{:S(2)}) copy-start(u32[32]{0:T(128)} %constant.157) | copy-start | bytes 388
  880.6 16.1 %copy-start.37 = (bf16[256]{0:T(256)(128)(2,1)S(1)}, bf16[256]{0:T(256)(128)(2,1)}, u32[]{:S(2)}) copy-start(bf16[256]{0:T(256)(128)(2,1)} %param.32) | copy-start | bytes 1540
  894.8 18.3 %copy-start.32 = (bf16[2048]{0:T(1024)(128)(2,1)S(1)}, bf16[2048]{0:T(1024)(128)(2,1)}, u32[]{:S(2)}) copy-start(bf16[2048]{0:T(1024)(128)(2,1)} %get-tuple-element.519) | copy-start | bytes 12292
  1216.1 6.7 copy-start.1
  1216.1 6.7 copy-start.8
  (13 other events, 14.1 us)
Sparse Core Ops, SparseCore 0:
  9.6 83.4 all-gather.13
  95.5 45.0 all-gather.15
  142.5 28.0 all-gather.17
  192.5 154.8 all-reduce.14
  349.1 53.2 all-gather.19
  403.8 80.7 all-gather.23
  486.4 54.3 all-gather.21
  575.3 154.9 all-reduce.16
  797.9 30.3 reduce-scatter.16
  832.0 41.1 reduce-scatter.10
  875.7 290.8 all-reduce.18
  1169.9 71.3 reduce-scatter.14
  1244.7 71.4 reduce-scatter.12
  1319.5 61.6 reduce-scatter.8
where the time goes:
time: 1400 us; the launch traced here: 1390 us
  waiting for transfers between devices  872 us (62%)
  matrix products  195 us (14%)
  blocking collectives  148 us (11%)
  other arithmetic  108 us (8%)
  local copies, waits for them, and re-layouts  41.9 us (3%)
  between operations  17.3 us (1%)
    psum x2, waiting for transfers between devices, branch_total(): lax.psum(jnp.dot(source, weight, preferred_element_type=jnp.float32).asty...  362 us
    psum x1, waiting for transfers between devices, input_total(): lax.psum(contract_cols(source, weight).astype(jnp.bfloat16), 'tensor')  155 us
    all_gather x1, waiting for transfers between devices, shards(): lax.all_gather(cotangent, 'tensor', axis=0, tiled=True)  66.3 us
    dot_general x4, matrix products, contract_rows(): lax.dot_general(left, right, (((0,), (0,)), ((), ())), preferred_element_...  56.6 us
    all_gather x1, waiting for transfers between devices, shards(): lax.all_gather(down_weight, 'dp', axis=1, tiled=True)  56.3 us
    reduce_scatter x1, waiting for transfers between devices, shards(): lax.psum_scatter(up_weight_grad.astype(jnp.bfloat16), 'dp', scatter_dimen...  53.5 us
    all_gather x1, waiting for transfers between devices, shards(): lax.all_gather(tokens, 'tensor', axis=0, tiled=True)  51.9 us
    dot_general x4, matrix products, contract_cols(): lax.dot_general(left, right, (((1,), (1,)), ((), ())), preferred_element_...  50 us
  transfers between devices with their start and end apart: 14, of which 10 were waited for; matrix products, arithmetic and copies ran while one was open for 17% of the time, Pallas kernels for 0%

commit v1 on v0

--- a/solution.py
+++ b/solution.py
@@ -7,6 +7,19 @@
 HD = 128
 LEN = 1024
 EPS = 1e-05
+
+
+def collect(value, axis, dim):
+    peers, index, rows = (lax.axis_size(axis), lax.axis_index(axis), value.shape[dim])
+    right = [(i, (i + 1) % peers) for i in range(peers)]
+    result = jnp.zeros((*value.shape[:dim], peers * rows, *value.shape[dim + 1 :]), value.dtype)
+    held = value
+    for lap in range(peers):
+        holder = (index - lap) % peers
+        result = lax.dynamic_update_slice_in_dim(result, held, holder * rows, axis=dim)
+        if lap < peers - 1:
+            held = lax.ppermute(held, axis, right)
+    return result
 
 
 def layer_norm(values, norm_gain, norm_shift):
@@ -189,7 +202,7 @@
     valid_own = lax.dynamic_slice_in_dim(valid_all, own_first, own_rows, 0)
     own_count = jnp.sum(valid_own)
     tokens_in, cotangent_in = (
-        lax.all_gather(tokens, "tensor", axis=0, tiled=True),
+        collect(tokens, "tensor", 0),
         lax.all_gather(cotangent, "tensor", axis=0, tiled=True),
     )
 

time: 1400 us -> 1340 us (0.957)
  waiting for transfers between devices: 872 us -> 823 us
    all_gather x1 -> x0, waiting for transfers between devices: 51.9 us -> none  [shards(): lax.all_gather(tokens, 'tensor', axis=0, tiled=True)]
    ppermute x0 -> x3, waiting for transfers between devices: none -> 44.7 us  [collect(): held = lax.ppermute(held, axis, right)]
    all_gather x1, waiting for transfers between devices: 41.3 us -> 0.02 us  [shards(): lax.all_gather(qkv_weight, 'dp', axis=0, tiled=True)]
  transfers between devices with their start and end apart: 14 -> 16, of which waited for: 10 -> 11; matrix products, arithmetic and copies ran while one was open for 17% -> 17% of each run, Pallas kernels for 0% -> 0%
where the time goes in v1:
time: 1340 us
  waiting for transfers between devices  823 us (61%)
  matrix products  195 us (15%)
  blocking collectives  147 us (11%)
  other arithmetic  103 us (8%)
  local copies, waits for them, and re-layouts  41.9 us (3%)
  between operations  17.5 us (1%)
    psum x2, waiting for transfers between devices, branch_total(): lax.psum(jnp.dot(source, weight, preferred_element_type=jnp.float32).asty...  362 us
    psum x1, waiting for transfers between devices, input_total(): lax.psum(contract_cols(source, weight).astype(jnp.bfloat16), 'tensor')  155 us
    all_gather x1, waiting for transfers between devices, shards(): lax.all_gather(cotangent, 'tensor', axis=0, tiled=True)  66.3 us
    all_gather x1, waiting for transfers between devices, shards(): lax.all_gather(down_weight, 'dp', axis=1, tiled=True)  56.1 us
    dot_general x4, matrix products, contract_rows(): lax.dot_general(left, right, (((0,), (0,)), ((), ())), preferred_element_...  56.1 us
    reduce_scatter x1, waiting for transfers between devices, shards(): lax.psum_scatter(up_weight_grad.astype(jnp.bfloat16), 'dp', scatter_dimen...  53.8 us
    dot_general x4, matrix products, contract_cols(): lax.dot_general(left, right, (((1,), (1,)), ((), ())), preferred_element_...  50 us
    reduce_scatter x1, waiting for transfers between devices, shards(): lax.psum_scatter(qkv_weight_grad.astype(jnp.bfloat16), 'dp', scatter_dime...  48.8 us
  transfers between devices with their start and end apart: 16, of which 11 were waited for; matrix products, arithmetic and copies ran while one was open for 17% of the time, Pallas kernels for 0%

profile of v1, /device:TPU:0, one launch (start us, length us, event | category | flops | bytes accessed | tf_op | source)
XLA Modules:
  0.0 1337.7 jit_solution(2003222213993349613)
XLA Ops:
  12.7 25.4 %collective-permute-done = bf16[256,2048]{1,0:T(8,128)(2,1)S(1)} collective-permute-done((bf16[256,2048]{1,0:T(8,128)(2,1)}, bf16[256,2048]{1,0:T(8,128)(2,1)S(1)}, u32[]{:S(2)}, u32[]{:S(2)}) %collective-permute-start) | collective-permute-done | bytes 1048608 | tf_op jit(solution)/shard_map/ppermute | solution.py:21
  38.9 9.5 all_gather.42
  48.5 15.7 %collective-permute-done.1 = bf16[256,2048]{1,0:T(8,128)(2,1)S(1)} collective-permute-done((bf16[256,2048]{1,0:T(8,128)(2,1)S(1)}, bf16[256,2048]{1,0:T(8,128)(2,1)S(1)}, u32[]{:S(2)}, u32[]{:S(2)}) %collective-permute-start.1) | collective-permute-done | bytes 1048608 | tf_op jit(solution)/shard_map/ppermute | solution.py:21
  65.7 8.8 all-gather.1
  74.5 8.9 all-gather
  93.4 12.5 add_convert_fusion.2
  105.9 5.0 squeeze.48
  112.4 22.4 %while.50 = (s32[]{:T(128)}, bf16[2,512,4,128]{3,2,1,0:T(4,128)(2,1)}, f32[2,4,512]{2,1,0:T(4,128)S(1)}, s32[2]{0:T(128)S(1)}, s32[]{:T(128)}, /*index=5*/bf16[1...) while((s32[]{:T(128)}, ...), condition=%wide.region_5.6_spmd.clone.clone, body=%wide.region_2.5_spmd.clone.clone.sunk | while | flops 1100217856 | bytes 39917828 | solution.py:81
  134.9 7.0 convolution_convert_fusion.6
  144.4 8.5 all-gather.4
  152.9 8.9 all-gather.3
  161.8 8.0 all-gather.2
  169.8 8.8 all-gather.5
  178.8 115.9 %all-reduce.15.cloned.1.call-done = bf16[1024,2048]{1,0:T(8,128)(2,1)} async-done(((bf16[1024,2048]{1,0:T(8,128)(2,1)}), bf16[1024,2048]{1,0:T(8,128)(2,1)}) %all-reduce.15.cloned.1.call-update) | async-done | bytes 4194320 | tf_op jit(solution)/shard_map/psum | solution.py:213
  294.8 11.2 fusion.84
  306.0 4.5 multiply_reduce_fusion.3
  311.7 4.0 subtract_multiply_fusion
  315.7 34.0 %all-gather.17.cloned.1.call-done = bf16[2048,2048]{1,0:T(8,128)(2,1)} async-done(((bf16[256,2048]{1,0:T(8,128)(2,1)}), bf16[2048,2048]{1,0:T(8,128)(2,1)}) %all-gather.17.cloned.1.call-update) | async-done | bytes 8388624 | tf_op jit(solution)/shard_map/all_gather | solution.py:175
  349.8 15.9 %fusion.69 = f32[1024,2048]{1,0:T(8,128)} fusion(bf16[2048,2048]{1,0:T(8,128)(2,1)} %all-gather.17.cloned.1.call-done, f32[1024,2048]{1,0:T(8,128)} %subtract_multiply_fusion, f32[2048]{0:T(1024)S(1)} %bitcast.153, f32[2048]{0:T(1024)S(1)} %bitcast.140), kind=kOutput, calls=%fused_computation.120 | convolution fusion | flops 8596226048 | bytes 25182208 | tf_op jit(solution)/shard_map/dot_general | solution.py:255
  365.7 66.3 %all-gather.21.cloned.1.call-done = bf16[1024,2048]{1,0:T(8,128)(2,1)} async-done(((bf16[256,2048]{1,0:T(8,128)(2,1)}), bf16[1024,2048]{1,0:T(8,128)(2,1)}) %all-gather.21.cloned.1.call-update) | async-done | bytes 4194320 | tf_op jit(solution)/shard_map/all_gather | solution.py:206
  431.9 56.1 %all-gather.19.cloned.1.call-done = bf16[2048,2048]{1,0:T(8,128)(2,1)} async-done(((bf16[2048,256]{1,0:T(8,128)(2,1)}), bf16[2048,2048]{1,0:T(8,128)(2,1)}) %all-gather.19.cloned.1.call-update) | async-done | bytes 8388624 | tf_op jit(solution)/shard_map/all_gather | solution.py:177
  488.1 19.2 %fusion.87 = (bf16[2048]{0:T(1024)(128)(2,1)}, bf16[1024,2048]{1,0:T(8,128)(2,1)S(1)}) fusion(f32[1024,2048]{1,0:T(8,128)} %fusion.69, f32[2048]{0:T(1024)S(1)} %reshape.277, bf16[2048,2048]{1,0:T(8,128)(2,1)} %all-gather.19.cloned.1.call-done, f32[1024]{0:T(1024)S(1)} %fusion.82, bf16[1024,2048]{1,0:T(8,128)(2,1)} %all-gather.21.cloned.1.call-done), kind=kOutput, calls=%fused_computation.171 | convolution fusion | flops 8642361344 | bytes 25182208 | tf_op jit(solution)/shard_map/dot_general | solution.py:50
  509.3 13.1 convolution_convert_fusion.4
  522.5 155.1 %all-reduce.17.cloned.1.call-done = bf16[1024,2048]{1,0:T(8,128)(2,1)} async-done(((bf16[1024,2048]{1,0:T(8,128)(2,1)}), bf16[1024,2048]{1,0:T(8,128)(2,1)}) %all-reduce.17.cloned.1.call-update) | async-done | bytes 4194320 | tf_op jit(solution)/shard_map/psum | solution.py:219
  677.5 6.0 multiply_reduce_fusion.5
  684.6 8.3 convert_multiply_fusion
  692.9 6.5 fusion.66
  699.5 41.1 %while.51 = (s32[]{:T(128)}, f32[1024,4,128]{0,2,1:T(8,128)S(1)}, f32[1024,4,128]{0,2,1:T(8,128)}, bf16[2,512,4,128]{3,1,2,0:T(8,128)(2,1)}, s32[2]{0:T(128)S(1)...) while((s32[]{:T(128)}, f32[1024,4,128]{0,2,1:T(8,128)S(1)}, ...), condition=%wide.region_15.16_spmd.clone.clone, body=%wide.region_13.15_spmd.clone.clone.sunk | while | flops 2720005632 | bytes 100202928 | solution.py:126
  710.2 4.0 multiply_reduce_fusion.8
  726.2 5.1 bitcast_add_fusion.5
  731.3 4.0 multiply_reduce_fusion.8
  745.0 7.4 convolution_convert_fusion.7
  752.5 16.3 %convolution_convert_fusion.5 = bf16[1024,2048]{1,0:T(8,128)(2,1)} fusion(bf16[2048,2048]{1,0:T(8,128)(2,1)} %all-gather.19.cloned.1.call-done, f32[1024,2048]{1,0:T(8,128)} %fusion.69, f32[2048]{0:T(1024)S(1)} %copy-done.30), kind=kOutput, calls=%fused_computation.86 | convolution fusion | flops 8613003264 | bytes 20979712 | tf_op jit(solution)/shard_map/dot_general | solution.py:214
  776.3 11.2 convolution_convert_fusion.3
  788.2 20.6 %convolution_convert_fusion = bf16[2048,2048]{1,0:T(8,128)(2,1)} fusion(bf16[1024,2048]{1,0:T(8,128)(2,1)} %all-gather.21.cloned.1.call-done, f32[1024]{0:T(1024)S(1)} %copy-done.28, f32[1024,2048]{1,0:T(8,128)} %fusion.69, f32[2048]{0:T(1024)S(1)} %copy-done.30), kind=kOutput, calls=%fused_computation.77 | convolution fusion | flops 8621391872 | bytes 20983808 | tf_op jit(solution)/shard_map/dot_general | solution.py:44
  809.5 14.6 %convolution_convert_fusion.1 = bf16[2048,2048]{1,0:T(8,128)(2,1)} fusion(bf16[1024,2048]{1,0:T(8,128)(2,1)} %copy-done.42, f32[1024,2048]{1,0:T(8,128)} %subtract_multiply_fusion, f32[2048]{0:T(1024)S(1)} %bitcast.154, f32[2048]{0:T(1024)S(1)} %bitcast.143), kind=kOutput, calls=%fused_computation.78 | convolution fusion | flops 8600420352 | bytes 20987904 | tf_op jit(solution)/shard_map/dot_general | solution.py:44
  826.0 13.5 %convolution_convert_fusion.2 = bf16[2048,3,512]{2,0,1:T(8,128)(2,1)} fusion(bf16[3,512,1024]{2,1,0:T(8,128)(2,1)S(1)} %bitcast.135, f32[2048]{0:T(1024)S(1)} %bitcast.152, f32[2048]{0:T(1024)S(1)} %bitcast.145, bf16[1024,2048]{1,0:T(8,128)(2,1)} %copy-done.1, f32[1024]{0:T(1024)S(1)} %copy-done.26, f32[1024]{0:T(1024)S(1)} %copy-done.22), kind=kOutput, calls=%fused_computation.81 | convolution fusion | flops 6458179584 | bytes 13656064 | tf_op jit(solution)/shard_map/dot_general | solution.py:44
  841.4 8.7 all-gather.6
  850.9 6.5 convert_element_type.197
  867.7 246.0 %all-reduce.19.cloned.1.call-done = (bf16[1024,2048]{1,0:T(8,128)(2,1)}, bf16[1024,2048]{1,0:T(8,128)(2,1)}) async-done(((bf16[1024,2048]{1,0:T(8,128)(2,1)}, bf16[1024,2048]{1,0:T(8,128)(2,1)}), (bf16[1024,2048]{1,0:T(8,128)(2,1)}, bf16[1024,2048]{1,0:T(8,128)(2,1)})) %all-reduce.19.cloned.1.call-update) | async-done | bytes 8388624 | tf_op jit(solution)/shard_map/psum | solution.py:213
  1117.1 5.6 fusion.52
  1122.7 40.4 %all-reduce.7 = (f32[1]{0:T(128)}, f32[1]{0:T(128)}, f32[1]{0:T(128)}, f32[1]{0:T(128)}, f32[1]{0:T(128)}, /*index=5*/f32[]{:T(128)}) all-reduce(f32[1]{0:T(128)} %bitcast.25, f32[1]{0:T(128)} %bitcast.26, f32[1]{0:T(128)} %bitcast.27, f32[1]{0:T(128)} %bitcast.28, ...), channel_id=1, replica_groups=mesh['dp'=8,'tensor'=4] {'dp','tensor'}, use_global_device_ids=true, to_apply=%region_47.48 | all-reduce | flops 6 | bytes 48 | tf_op jit(solution)/shard_map/psum | solution.py:228
  1163.2 6.7 convert_element_type.225
  1172.9 5.0 dynamic-slice_reduce_fusion.3
  1177.9 24.2 %all-reduce.9 = (bf16[2048]{0:T(1024)(128)(2,1)S(1)}, bf16[2048]{0:T(1024)(128)(2,1)S(1)}, bf16[2048]{0:T(1024)(128)(2,1)S(1)}, bf16[2048]{0:T(1024)(128)(2,1)S(...) all-reduce(bf16[2048]{0:T(1024)(128)(2,1)S(1)} %get-tuple-element.5, ...), channel_id=2, replica_groups=mesh['dp'=8,'tensor'=4] {'dp'}, use_global_device_ids=true, to_apply=%region_20.21.clone | all-reduce | flops 14336 | bytes 57344
  1209.6 53.8 %reduce-scatter.13.cloned.1.call-done = bf16[256,2048]{1,0:T(8,128)(2,1)} async-done(((bf16[2048,2048]{1,0:T(8,128)(2,1)}), bf16[256,2048]{1,0:T(8,128)(2,1)}) %reduce-scatter.13.cloned.1.call-update) | async-done | bytes 1048592 | tf_op jit(solution)/shard_map/reduce_scatter | solution.py:325
  1266.6 12.5 all-reduce.8
  1279.6 48.8 %reduce-scatter.9.cloned.1.call-done = bf16[256,3,512]{2,0,1:T(8,128)(2,1)} async-done(((bf16[2048,3,512]{2,0,1:T(8,128)(2,1)}), bf16[256,3,512]{2,0,1:T(8,128)(2,1)}) %reduce-scatter.9.cloned.1.call-update) | async-done | bytes 786448 | tf_op jit(solution)/shard_map/reduce_scatter | solution.py:316
  (258 shorter events, 115.0 us)
Async XLA Ops:
  7.2 85.7 %all-gather.13.cloned.1.call-start = ((), (), s32[]{:S(2)}) async-start(), calls=%async_computation.5 | async-start | bytes 7077888 | tf_op jit(solution)/shard_map/all_gather | solution.py:169
  9.5 125.3 %all-gather.15.cloned.1.call-start = ((), (), s32[]{:S(2)}) async-start(), calls=%async_computation.6 | async-start | bytes 2359296 | tf_op jit(solution)/shard_map/all_gather | solution.py:171
  9.6 28.5 %collective-permute-start = (bf16[256,2048]{1,0:T(8,128)(2,1)}, bf16[256,2048]{1,0:T(8,128)(2,1)S(1)}, u32[]{:S(2)}, u32[]{:S(2)}) collective-permute-start(bf16[256,2048]{1,0:T(8,128)(2,1)} %param.19), channel_id=1, source_target_pairs={{0,1},{1,2},{2,3},{3,0},{4,5},{5,6},{6,7},{7,4},{8,9},{9,10},{10,1... | collective-permute-start | bytes 3145736 | tf_op jit(solution)/shard_map/ppermute | solution.py:21
  38.1 26.1 %collective-permute-start.1 = (bf16[256,2048]{1,0:T(8,128)(2,1)S(1)}, bf16[256,2048]{1,0:T(8,128)(2,1)S(1)}, u32[]{:S(2)}, u32[]{:S(2)}) collective-permute-start(bf16[256,2048]{1,0:T(8,128)(2,1)S(1)} %collective-permute-done), channel_id=1, source_target_pairs={{0,1},{1,2},{2,3},{3,0},{4,5},{5,6},{6,7},{7,4},{8,9},{9,10},{10,1... | collective-permute-start | bytes 3145736 | tf_op jit(solution)/shard_map/ppermute | solution.py:21
  38.1 256.6 %all-reduce.15.cloned.1.call-start = ((), (), s32[]{:S(2)}) async-start(), calls=%async_computation.7 | async-start | bytes 8388608 | tf_op jit(solution)/shard_map/psum | solution.py:213
  64.2 25.3 %collective-permute-start.2 = (bf16[256,2048]{1,0:T(8,128)(2,1)S(1)}, bf16[256,2048]{1,0:T(8,128)(2,1)S(1)}, u32[]{:S(2)}, u32[]{:S(2)}) collective-permute-start(bf16[256,2048]{1,0:T(8,128)(2,1)S(1)} %collective-permute-done.1), channel_id=1, source_target_pairs={{0,1},{1,2},{2,3},{3,0},{4,5},{5,6},{6,7},{7,4},{8,9},{9,10},{10,1... | collective-permute-start | bytes 3145736 | tf_op jit(solution)/shard_map/ppermute | solution.py:21
  74.5 18.3 %copy-start.31 = (f32[8,1,256]{2,1,0:T(1,128)}, f32[8,1,256]{2,1,0:T(1,128)S(1)}, u32[]{:S(2)}) copy-start(f32[8,1,256]{2,1,0:T(1,128)S(1)} %convert_element_type.259) | copy-start | bytes 24580
  83.5 9.4 copy-start.23
  118.9 3.2 copy-start.17
  129.9 3.2 copy-start.17
  134.8 7.7 copy-start.3
  134.8 7.7 copy-start.7
  134.8 9.5 copy-start.37
  134.8 9.5 copy-start.38
  134.8 9.5 copy-start.39
  134.8 35.0 %copy-start.36 = (bf16[128,2]{0,1:T(2,128)(2,1)S(1)}, bf16[128,2]{0,1:T(2,128)(2,1)}, u32[]{:S(2)}) copy-start(bf16[128,2]{0,1:T(2,128)(2,1)} %param.30) | copy-start | bytes 1540
  141.8 207.9 %all-gather.17.cloned.1.call-start = ((), (), s32[]{:S(2)}) async-start(), calls=%async_computation.8 | async-start | bytes 9437184 | tf_op jit(solution)/shard_map/all_gather | solution.py:175
  142.4 289.5 %all-gather.21.cloned.1.call-start = ((), (), s32[]{:S(2)}) async-start(), calls=%async_computation.10 | async-start | bytes 5242880 | tf_op jit(solution)/shard_map/all_gather | solution.py:206
  143.0 345.0 %all-gather.19.cloned.1.call-start = ((), (), s32[]{:S(2)}) async-start(), calls=%async_computation.9 | async-start | bytes 9437184 | tf_op jit(solution)/shard_map/all_gather | solution.py:177
  143.6 533.9 %all-reduce.17.cloned.1.call-start = ((), (), s32[]{:S(2)}) async-start(), calls=%async_computation.11 | async-start | bytes 8388608 | tf_op jit(solution)/shard_map/psum | solution.py:219
  152.9 196.9 %copy-start.33 = (f32[8,1,256]{2,1,0:T(1,128)}, f32[8,1,256]{2,1,0:T(1,128)S(1)}, u32[]{:S(2)}) copy-start(f32[8,1,256]{2,1,0:T(1,128)S(1)} %convert_element_type.262) | copy-start | bytes 24580
  161.8 521.7 %copy-start.19 = (f32[8,1,256]{2,1,0:T(1,128)}, f32[8,1,256]{2,1,0:T(1,128)S(1)}, u32[]{:S(2)}) copy-start(f32[8,1,256]{2,1,0:T(1,128)S(1)} %convert_element_type.261) | copy-start | bytes 24580
  178.8 309.3 %copy-start.29 = (f32[2048]{0:T(1024)}, f32[2048]{0:T(1024)S(1)}, u32[]{:S(2)}) copy-start(f32[2048]{0:T(1024)S(1)} %reshape.277) | copy-start | bytes 24580
  178.8 504.7 %copy-start.27 = (f32[1024]{0:T(1024)}, f32[1024]{0:T(1024)S(1)}, u32[]{:S(2)}) copy-start(f32[1024]{0:T(1024)S(1)} %fusion.82) | copy-start | bytes 12292
  306.0 5.8 copy-start
  522.4 342.1 %reduce-scatter.17.cloned.1.call-start = ((), (), s32[]{:S(2)}) async-start(), calls=%async_computation.16 | async-start | bytes 36864
  677.5 6.0 copy-start.6
  677.5 7.1 copy-start.12
  692.9 6.5 copy-start.5
  702.8 3.5 copy-start.11
  706.3 3.8 copy-start.8
  714.2 3.9 copy-start.4
  722.7 3.5 copy-start.11
  726.2 5.1 copy-start.8
  735.3 3.9 copy-start.4
  742.0 10.5 copy-start.30
  743.8 25.0 %copy-start.10 = (bf16[1024,4,128]{2,0,1:T(8,128)(2,1)}, bf16[1024,4,128]{2,0,1:T(8,128)(2,1)S(1)}, u32[]{:S(2)}) copy-start(bf16[1024,4,128]{2,0,1:T(8,128)(2,1)S(1)} %copy.113) | copy-start | bytes 3145732
  744.9 121.0 %reduce-scatter.11.cloned.1.call-start = ((), (), s32[]{:S(2)}) async-start(), calls=%async_computation.13 | async-start | bytes 2359296 | tf_op jit(solution)/shard_map/reduce_scatter | solution.py:322
  752.4 361.3 %all-reduce.19.cloned.1.call-start = ((), (), s32[]{:S(2)}) async-start(), calls=%async_computation.17 | async-start | bytes 16777216 | tf_op jit(solution)/shard_map/psum | solution.py:213
  752.5 16.4 %copy-start.15 = (bf16[2,512,4,128]{3,1,2,0:T(8,128)(2,1)S(1)}, bf16[2,512,4,128]{3,1,2,0:T(8,128)(2,1)}, u32[]{:S(2)}) copy-start(bf16[2,512,4,128]{3,1,2,0:T(8,128)(2,1)} %get-tuple-element.174) | copy-start | bytes 3145732
  787.5 419.3 %reduce-scatter.15.cloned.1.call-start = ((), (), s32[]{:S(2)}) async-start(), calls=%async_computation.15 | async-start | bytes 9437184 | tf_op jit(solution)/shard_map/reduce_scatter | solution.py:331
  808.8 454.6 %reduce-scatter.13.cloned.1.call-start = ((), (), s32[]{:S(2)}) async-start(), calls=%async_computation.14 | async-start | bytes 9437184 | tf_op jit(solution)/shard_map/reduce_scatter | solution.py:325
  824.1 504.3 %reduce-scatter.9.cloned.1.call-start = ((), (), s32[]{:S(2)}) async-start(), calls=%async_computation.12 | async-start | bytes 7077888 | tf_op jit(solution)/shard_map/reduce_scatter | solution.py:316
  826.0 13.5 %copy-start.41 = (u32[32]{0:T(128)S(1)}, u32[32]{0:T(128)}, u32[]{:S(2)}) copy-start(u32[32]{0:T(128)} %constant.190) | copy-start | bytes 388
  826.0 15.4 %copy-start.40 = (bf16[256]{0:T(256)(128)(2,1)S(1)}, bf16[256]{0:T(256)(128)(2,1)}, u32[]{:S(2)}) copy-start(bf16[256]{0:T(256)(128)(2,1)} %param.32) | copy-start | bytes 1540
  839.5 17.9 %copy-start.35 = (bf16[2048]{0:T(1024)(128)(2,1)S(1)}, bf16[2048]{0:T(1024)(128)(2,1)}, u32[]{:S(2)}) copy-start(bf16[2048]{0:T(1024)(128)(2,1)} %get-tuple-element.519) | copy-start | bytes 12292
  1163.2 6.7 copy-start.2
  1163.2 6.7 copy-start.9
  (18 other events, 27.1 us)
Sparse Core Ops, SparseCore 0:
  10.4 49.5 all-gather.12
  61.9 28.0 all-gather.14
  142.0 152.7 all-reduce.14
  296.5 53.2 all-gather.16
  351.2 80.7 all-gather.20
  433.7 54.3 all-gather.18
  522.5 154.9 all-reduce.16
  745.0 30.2 reduce-scatter.16
  779.2 41.1 reduce-scatter.10
  822.8 290.8 all-reduce.18
  1117.2 71.2 reduce-scatter.14
  1191.8 71.4 reduce-scatter.12
  1266.7 61.6 reduce-scatter.8
